TPU v7x, 512 devices: a whole 4x8x8 slice. The times are simulated.
512 devices in a mesh: seq: 64 (over y, z), trk: 8 (over x, core).
Axes of the slice: x: 4, y: 8, z: 8, core: 2. Of those that a mesh axis runs over, the one named last changes fastest.
Arguments:
- embeddings: bfloat16 [4, 8192, 1920], P(None, 'seq', 'trk'), may hold values from -16 to 16
- head: bfloat16 [1920, 4096], P(None, 'trk'), may hold values from -0.125 to 0.125
- exon_starts: int32 [4, 128, 8], replicated, may hold values from 0 to 8184, as said below
- exon_lengths: int32 [4, 128, 8], replicated, may hold values from 1 to 8, as said below
- gene_owner: int32 [4, 128], replicated, may hold values from 0 to 63, as said below
- gene_targets: float32 [4, 256, 4096], P(None, 'seq', 'trk'), may hold values from 2 to 400, as said below
Outputs:
- gene_pred: float32 [4, 256, 4096], P(None, 'seq', 'trk')
- loss: float32 [4, 4096], P(None, 'trk')
- grad_head: float32 [1920, 4096], P('seq', 'trk')
Inputs may be any that keep to these rules, and one draw needn't show every extreme that they name: `exon_starts`: each gene has 8 exon blocks; blocks may intersect. Some block of each window starts at 0 and some at 8184. `exon_lengths`: some block of each window has length 8. `gene_owner`: in each window no owner holds more than 4 genes, and some owner holds exactly 4. `gene_targets`: entries of empty slots are read by nothing.
All inputs are finite; a program needn't handle non-finite values.
Results may differ from a plain program's by a relative error of at most 0.0041.
Values may be sent and summed in bfloat16 or wider, within the bound.
No kernel may reach another device: no remote copies, remote signals or barrier semaphores. Data moves between devices by JAX's collectives and lax.ppermute only.
A program may use at most 64 MiB of HBM per device.

v0:
```python
import jax
import jax.numpy as jnp
from jax import lax
from jax.sharding import PartitionSpec as P


def slot_table(gene_owner, capacity):
    genes = gene_owner.shape[1]
    same = gene_owner[:, :, None] == gene_owner[:, None, :]
    earlier = jnp.arange(genes)[None, :] < jnp.arange(genes)[:, None]
    ahead = jnp.sum((same & earlier[None]).astype(jnp.int32), axis=2)
    return gene_owner * capacity + ahead


def coverage(starts, lengths, positions):
    where_bin = positions[None, None, None, :]
    inside = (where_bin >= starts[..., None]) & (where_bin < (starts + lengths)[..., None])
    return jnp.sum(inside.astype(jnp.float32), axis=2)


def fold_sources(received):
    return jnp.sum(received, axis=1)


def per_device(embeddings, head, exon_starts, exon_lengths, gene_owner, gene_targets):
    seq_devices = lax.axis_size("seq")
    seq_place = lax.axis_index("seq")
    windows, bin_dev, _ = embeddings.shape
    genes = gene_owner.shape[1]
    capacity = gene_targets.shape[1]
    slot_total = seq_devices * capacity
    whole = lax.all_gather(embeddings, "trk", axis=2, tiled=True)
    logits = jnp.einsum("wbd,dt->wbt", whole, head, preferred_element_type=jnp.float32)
    pred = jax.nn.softplus(logits).astype(jnp.bfloat16)
    positions = seq_place * bin_dev + jnp.arange(bin_dev, dtype=jnp.int32)
    cover = coverage(exon_starts, exon_lengths, positions)
    slot_of = slot_table(gene_owner, capacity)
    onehot = (slot_of[..., None] == jnp.arange(slot_total, dtype=jnp.int32)).astype(jnp.float32)
    member = jnp.einsum("wgs,wgb->wsb", onehot, cover, precision=lax.Precision.HIGHEST).astype(
        jnp.bfloat16
    )
    valid = jnp.sum(onehot, axis=1)
    valid_here = lax.dynamic_slice_in_dim(valid, seq_place * capacity, capacity, 1)
    targets_here = gene_targets * valid_here[..., None]
    target_part = jnp.sum(targets_here, axis=1)
    partial_value = jnp.einsum("wsb,wbt->wst", member, pred, preferred_element_type=jnp.float32)
    blocks = partial_value.reshape(windows, seq_devices, capacity, partial_value.shape[2])
    gene_here = fold_sources(lax.all_to_all(blocks, "seq", split_axis=1, concat_axis=1, tiled=True))
    safe = jnp.where(valid_here[..., None] > 0, gene_here, 1.0)
    fit_part = jnp.sum(targets_here * jnp.log(safe), axis=1)
    total, target_sum, fit = lax.psum((jnp.sum(gene_here, axis=1), target_part, fit_part), "seq")
    scale_rows = (genes / target_sum)[:, None, :]
    gene_grad = (
        scale_rows
        * (
            valid_here[..., None] * (0.2 + 0.8 * target_sum / total)[:, None, :]
            - targets_here / safe
        )
    ).astype(jnp.bfloat16)
    bin_grad = jnp.einsum(
        "wsb,wst->wbt",
        member,
        lax.all_gather(gene_grad, "seq", axis=1, tiled=True),
        preferred_element_type=jnp.float32,
    )
    logit_grad = (bin_grad * jax.nn.sigmoid(logits)).astype(jnp.bfloat16)
    grad_head = lax.psum_scatter(
        jnp.einsum("wbd,wbt->dt", whole, logit_grad, preferred_element_type=jnp.float32),
        "seq",
        scatter_dimension=0,
        tiled=True,
    )
    log_total = jnp.log(total)
    loss = (-fit + target_sum * log_total + 0.2 * (total - target_sum * log_total)) / target_sum
    return (gene_here, loss, grad_head)


def solution(mesh):
    return jax.shard_map(
        per_device,
        mesh=mesh,
        in_specs=(P(None, "seq", "trk"), P(None, "trk"), P(), P(), P(), P(None, "seq", "trk")),
        out_specs=(P(None, "seq", "trk"), P(None, "trk"), P("seq", "trk")),
        check_vma=False,
    )
```

profile of v0, /device:TPU:2, one launch (start us, length us, event | category | flops | bytes accessed | tf_op | source)
XLA Modules:
  0.0 664.6 jit_solution(17121487797619391338)
XLA Ops:
  7.2 0.0 copy-start
  7.2 0.0 all-gather.3.cloned.1.call-start
  7.2 0.7 all-gather.3.cloned.1.call-update
  7.9 0.8 copy.28
  8.8 0.7 add.46
  9.5 0.1 copy.29
  9.7 1.0 convert_reduce_fusion.2
  10.7 0.7 multiply_add_fusion
  11.4 1.4 convert_reduce_fusion
  12.8 0.4 convolution_convert_fusion
  13.2 30.7 %all-gather.3.cloned.1.call-done = bf16[4,128,1920]{1,2,0:T(8,128)(2,1)} async-done(((bf16[4,128,240]{1,2,0:T(8,128)(2,1)}), bf16[4,128,1920]{1,2,0:T(8,128)(2,1)}) %all-gather.3.cloned.1.call-update) | async-done | bytes 1966096 | tf_op jit(solution)/shard_map/all_gather | solution.py:32
  43.9 0.0 copy-done
  43.9 2.8 fusion.13
  46.8 2.2 fusion.9
  48.9 2.9 reshape.35
  51.8 3.5 copy.30
  55.4 13.6 %all-to-all-start = ((f32[4,64,4,512]{3,2,0,1:T(4,128)}), f32[4,64,4,512]{3,2,0,1:T(4,128)}, u32[]{:S(2)}, u32[]{:S(2)}) async-start(f32[4,64,4,512]{3,2,0,1:T(4,128)} %copy.30), calls=%async_computation | async-start | bytes 4194304 | tf_op jit(solution)/shard_map/all_to_all | solution.py:48
  68.9 0.0 copy-start.2
  68.9 0.0 all-gather.5.cloned.1.call-start
  69.0 0.1 convert_reduce_fusion.1
  69.1 0.1 broadcast_compare_fusion
  69.2 51.5 %all-to-all-done = f32[4,64,4,512]{3,2,0,1:T(4,128)} async-done(((f32[4,64,4,512]{3,2,0,1:T(4,128)}), f32[4,64,4,512]{3,2,0,1:T(4,128)}, u32[]{:S(2)}, u32[]{:S(2)}) %all-to-all-start) | async-done | bytes 2097184 | tf_op jit(solution)/shard_map/all_to_all | solution.py:48
  120.7 2.1 fusion.20
  122.7 0.0 copy-start.1
  122.8 0.0 copy-done.2
  122.8 0.1 multiply_reduce_fusion
  122.9 282.3 %all-reduce.1 = (f32[4,512]{1,0:T(4,128)S(1)}, f32[4,512]{1,0:T(4,128)S(1)}, f32[4,512]{1,0:T(4,128)S(1)}) all-reduce(f32[4,512]{1,0:T(4,128)S(1)} %get-tuple-element.18, f32[4,512]{1,0:T(4,128)S(1)} %get-tuple-element.15, f32[4,512]{1,0:T(4,128)S(1)} %get-tuple-element.17), channel_id=1, replica_groups=mesh['seq'=64,'trk'=8] {'seq'}, use_global_device_ids=true, to_apply=%region_7.8 | all-reduce | flops 6144 | bytes 49152 | tf_op jit(solution)/shard_map/psum | solution.py:51
  405.2 0.6 fusion.16
  405.8 0.1 multiply_convert_fusion
  405.9 0.6 copy.31
  406.5 0.0 all-gather.5.cloned.1.call-update
  406.5 0.0 all-reduce.4.cloned.1.call-start
  406.6 76.9 %all-gather.5.cloned.1.call-done = bf16[4,256,512]{2,0,1:T(4,128)(2,1)} async-done(((bf16[4,4,512]{2,0,1:T(4,128)(2,1)}), bf16[4,256,512]{2,0,1:T(4,128)(2,1)}) %all-gather.5.cloned.1.call-update) | async-done | bytes 1048592 | tf_op jit(solution)/shard_map/all_gather | solution.py:63
  483.5 5.5 convolution_bitcast_fusion
  489.0 0.0 copy-done.1
  489.0 0.0 all-reduce.4.cloned.1.call-update
  489.0 1.3 dynamic-slice
  490.9 165.2 %all-reduce.4.cloned.1.call-done = f32[1920,512]{0,1:T(8,128)} async-done(((f32[1920,512]{0,1:T(8,128)}), f32[1920,512]{0,1:T(8,128)}) %all-reduce.4.cloned.1.call-update) | async-done | bytes 3932176
  656.1 1.2 constant_dynamic-slice_fusion
  657.3 0.8 copy.35
  (2 shorter events, 0.0 us)
Async XLA Ops:
  7.2 36.7 %copy-start = (bf16[1920,512]{1,0:T(8,128)(2,1)S(1)}, bf16[1920,512]{1,0:T(8,128)(2,1)}, u32[]{:S(2)}) copy-start(bf16[1920,512]{1,0:T(8,128)(2,1)} %param.7) | copy-start | bytes 5898244
  7.2 36.7 %all-gather.3.cloned.1.call-start = ((), (), s32[]{:S(2)}) async-start(), calls=%async_computation.1 | async-start | bytes 2211840 | tf_op jit(solution)/shard_map/all_gather | solution.py:32
  55.4 65.3 %all-to-all-start = ((f32[4,64,4,512]{3,2,0,1:T(4,128)}), f32[4,64,4,512]{3,2,0,1:T(4,128)}, u32[]{:S(2)}, u32[]{:S(2)}) async-start(f32[4,64,4,512]{3,2,0,1:T(4,128)} %copy.30), calls=%async_computation | async-start | bytes 4194304 | tf_op jit(solution)/shard_map/all_to_all | solution.py:48
  68.9 53.8 %copy-start.2 = (f32[4,4,512]{2,1,0:T(4,128)S(1)}, f32[4,4,512]{2,1,0:T(4,128)}, u32[]{:S(2)}) copy-start(f32[4,4,512]{2,1,0:T(4,128)} %param.11) | copy-start | bytes 98308
  68.9 414.6 %all-gather.5.cloned.1.call-start = ((), (), s32[]{:S(2)}) async-start(), calls=%async_computation.2 | async-start | bytes 1064960 | tf_op jit(solution)/shard_map/all_gather | solution.py:63
  122.7 366.2 %copy-start.1 = (f32[4,4,512]{2,1,0:T(4,128)}, f32[4,4,512]{2,1,0:T(4,128)S(1)}, u32[]{:S(2)}) copy-start(f32[4,4,512]{2,1,0:T(4,128)S(1)} %get-tuple-element.16) | copy-start | bytes 98308
  406.5 249.6 %all-reduce.4.cloned.1.call-start = ((), (), s32[]{:S(2)}) async-start(), calls=%async_computation.3 | async-start | bytes 7864320
Sparse Core Ops, SparseCore 0:
  10.1 33.7 all-gather.2
  406.7 76.7 all-gather.4
  489.1 166.9 all-reduce.3
where the time goes:
time: 665 us
  waiting for transfers between devices  325 us (49%)
  blocking collectives  282 us (42%)
  between operations  14.5 us (2%)
  starting transfers between devices  13.7 us (2%)
  local copies, waits for them, and re-layouts  11.2 us (2%)
  matrix products  10.9 us (2%)
  other arithmetic  7 us (1%)
    psum x1, blocking collectives, per_device(): lax.psum((jnp.sum(gene_here, axis=1), target_part, fit_part), 'seq')  282 us
    unnamed x4, waiting for transfers between devices  166 us
    all_gather x1, waiting for transfers between devices, per_device(): lax.all_gather(gene_grad, 'seq', axis=1, tiled=True)  76.9 us
    all_to_all x1, waiting for transfers between devices, per_device(): lax.all_to_all(blocks, 'seq', split_axis=1, concat_axis=1, tiled=True)  51.5 us
    all_gather x1, waiting for transfers between devices, per_device(): whole = lax.all_gather(embeddings, 'trk', axis=2, tiled=True)  30.7 us
    all_to_all x1, starting transfers between devices, per_device(): lax.all_to_all(blocks, 'seq', split_axis=1, concat_axis=1, tiled=True)  13.6 us
  transfers between devices with their start and end apart: 4, of which 4 were waited for; matrix products, arithmetic and copies ran while one was open for 1% of the time, Pallas kernels for 0%

commit v1 on v0

--- a/solution.py
+++ b/solution.py
@@ -60,7 +60,9 @@
     bin_grad = jnp.einsum(
         "wsb,wst->wbt",
         member,
-        lax.all_gather(gene_grad, "seq", axis=1, tiled=True),
+        jnp.concatenate(
+            lax.all_to_all(jnp.stack([gene_grad] * lax.axis_size("seq")), "seq", 0, 0), axis=1
+        ),
         preferred_element_type=jnp.float32,
     )
     logit_grad = (bin_grad * jax.nn.sigmoid(logits)).astype(jnp.bfloat16)

time: 665 us -> 615 us (0.925)
  waiting for transfers between devices: 325 us -> 246 us
  blocking collectives: 282 us -> 311 us
    all_gather x1 -> x0, waiting for transfers between devices: 76.9 us -> none  [per_device(): lax.all_gather(gene_grad, 'seq', axis=1, tiled=True)]
    all_to_all x0 -> x1, blocking collectives: none -> 26.6 us  [per_device(): lax.all_to_all(jnp.stack([gene_grad] * lax.axis_size('seq')), 'seq', 0, 0)]
    unnamed x4 -> x3, waiting for transfers between devices: 166 us -> 164 us
  transfers between devices with their start and end apart: 4 -> 3, of which waited for: 4 -> 3; matrix products, arithmetic and copies ran while one was open for 1% -> 1% of each run, Pallas kernels for 0% -> 0%
where the time goes in v1:
time: 615 us
  blocking collectives  311 us (51%)
  waiting for transfers between devices  246 us (40%)
  between operations  14.8 us (2%)
  starting transfers between devices  13.6 us (2%)
  local copies, waits for them, and re-layouts  11.1 us (2%)
  matrix products  10.9 us (2%)
  other arithmetic  7 us (1%)
    psum x1, blocking collectives, per_device(): lax.psum((jnp.sum(gene_here, axis=1), target_part, fit_part), 'seq')  285 us
    unnamed x3, waiting for transfers between devices  164 us
    all_to_all x1, waiting for transfers between devices, per_device(): lax.all_to_all(blocks, 'seq', split_axis=1, concat_axis=1, tiled=True)  51.5 us
    all_gather x1, waiting for transfers between devices, per_device(): whole = lax.all_gather(embeddings, 'trk', axis=2, tiled=True)  30.7 us
    all_to_all x1, blocking collectives, per_device(): lax.all_to_all(jnp.stack([gene_grad] * lax.axis_size('seq')), 'seq', 0, 0)  26.6 us
    all_to_all x1, starting transfers between devices, per_device(): lax.all_to_all(blocks, 'seq', split_axis=1, concat_axis=1, tiled=True)  13.6 us
  transfers between devices with their start and end apart: 3, of which 3 were waited for; matrix products, arithmetic and copies ran while one was open for 1% of the time, Pallas kernels for 0%

profile of v1, /device:TPU:2, one launch (start us, length us, event | category | flops | bytes accessed | tf_op | source)
XLA Modules:
  0.0 614.8 jit_solution(17201438990222543362)
XLA Ops:
  7.2 0.0 copy-start
  7.2 0.0 all-gather.2.cloned.1.call-start
  7.2 0.7 all-gather.2.cloned.1.call-update
  7.9 0.8 copy.26
  8.8 0.7 add.46
  9.5 0.1 copy.27
  9.7 1.0 convert_reduce_fusion.2
  10.7 0.7 multiply_add_fusion
  11.4 1.4 convert_reduce_fusion
  12.8 0.4 convolution_convert_fusion
  13.2 30.7 %all-gather.2.cloned.1.call-done = bf16[4,128,1920]{1,2,0:T(8,128)(2,1)} async-done(((bf16[4,128,240]{1,2,0:T(8,128)(2,1)}), bf16[4,128,1920]{1,2,0:T(8,128)(2,1)}) %all-gather.2.cloned.1.call-update) | async-done | bytes 1966096 | tf_op jit(solution)/shard_map/all_gather | solution.py:32
  43.9 0.0 copy-done
  43.9 2.8 fusion.13
  46.8 2.2 fusion.9
  48.9 2.9 reshape.43
  51.8 3.5 copy.28
  55.4 13.6 %all-to-all-start = ((f32[4,64,4,512]{3,2,0,1:T(4,128)}), f32[4,64,4,512]{3,2,0,1:T(4,128)}, u32[]{:S(2)}, u32[]{:S(2)}) async-start(f32[4,64,4,512]{3,2,0,1:T(4,128)} %copy.28), calls=%async_computation | async-start | bytes 4194304 | tf_op jit(solution)/shard_map/all_to_all | solution.py:48
  68.9 0.0 copy-start.2
  68.9 0.0 all-reduce.4.cloned.1.call-start
  69.0 0.1 convert_reduce_fusion.1
  69.1 0.1 broadcast_compare_fusion
  69.2 51.5 %all-to-all-done = f32[4,64,4,512]{3,2,0,1:T(4,128)} async-done(((f32[4,64,4,512]{3,2,0,1:T(4,128)}), f32[4,64,4,512]{3,2,0,1:T(4,128)}, u32[]{:S(2)}, u32[]{:S(2)}) %all-to-all-start) | async-done | bytes 2097184 | tf_op jit(solution)/shard_map/all_to_all | solution.py:48
  120.7 2.1 fusion.20
  122.7 0.0 copy-start.1
  122.7 0.0 copy-done.2
  122.8 0.1 multiply_reduce_fusion
  122.9 284.7 %all-reduce.1 = (f32[4,512]{1,0:T(4,128)S(1)}, f32[4,512]{1,0:T(4,128)S(1)}, f32[4,512]{1,0:T(4,128)S(1)}) all-reduce(f32[4,512]{1,0:T(4,128)S(1)} %get-tuple-element.18, f32[4,512]{1,0:T(4,128)S(1)} %get-tuple-element.15, f32[4,512]{1,0:T(4,128)S(1)} %get-tuple-element.17), channel_id=1, replica_groups=mesh['seq'=64,'trk'=8] {'seq'}, use_global_device_ids=true, to_apply=%region_7.8 | all-reduce | flops 6144 | bytes 49152 | tf_op jit(solution)/shard_map/psum | solution.py:51
  407.6 0.6 fusion.16
  408.2 0.1 multiply_convert_fusion
  408.3 0.5 stack.2
  408.8 26.6 %all_to_all.10 = bf16[64,4,4,512]{3,1,2,0:T(4,128)(2,1)} all-to-all(bf16[64,4,4,512]{3,1,2,0:T(4,128)(2,1)S(1)} %stack.2), channel_id=1, replica_groups=mesh['seq'=64,'trk'=8] {'seq'}, dimensions={0} | all-to-all | bytes 2097152 | tf_op jit(solution)/shard_map/all_to_all | solution.py:64
  435.5 5.5 convolution_bitcast_fusion
  441.0 0.0 copy-done.1
  441.0 0.0 all-reduce.4.cloned.1.call-update
  441.0 1.3 dynamic-slice
  442.9 163.1 %all-reduce.4.cloned.1.call-done = f32[1920,512]{0,1:T(8,128)} async-done(((f32[1920,512]{0,1:T(8,128)}), f32[1920,512]{0,1:T(8,128)}) %all-reduce.4.cloned.1.call-update) | async-done | bytes 3932176
  606.0 1.2 constant_dynamic-slice_fusion
  607.2 0.8 copy.33
  (3 shorter events, 0.0 us)
Async XLA Ops:
  7.2 36.7 %copy-start = (bf16[1920,512]{1,0:T(8,128)(2,1)S(1)}, bf16[1920,512]{1,0:T(8,128)(2,1)}, u32[]{:S(2)}) copy-start(bf16[1920,512]{1,0:T(8,128)(2,1)} %param.7) | copy-start | bytes 5898244
  7.2 36.7 %all-gather.2.cloned.1.call-start = ((), (), s32[]{:S(2)}) async-start(), calls=%async_computation.2 | async-start | bytes 2211840 | tf_op jit(solution)/shard_map/all_gather | solution.py:32
  55.4 65.3 %all-to-all-start = ((f32[4,64,4,512]{3,2,0,1:T(4,128)}), f32[4,64,4,512]{3,2,0,1:T(4,128)}, u32[]{:S(2)}, u32[]{:S(2)}) async-start(f32[4,64,4,512]{3,2,0,1:T(4,128)} %copy.28), calls=%async_computation | async-start | bytes 4194304 | tf_op jit(solution)/shard_map/all_to_all | solution.py:48
  68.9 53.8 %copy-start.2 = (f32[4,4,512]{2,1,0:T(4,128)S(1)}, f32[4,4,512]{2,1,0:T(4,128)}, u32[]{:S(2)}) copy-start(f32[4,4,512]{2,1,0:T(4,128)} %param.11) | copy-start | bytes 98308
  68.9 537.1 %all-reduce.4.cloned.1.call-start = ((), (), s32[]{:S(2)}) async-start(), calls=%async_computation.3 | async-start | bytes 7864320
  122.7 318.2 %copy-start.1 = (f32[4,4,512]{2,1,0:T(4,128)}, f32[4,4,512]{2,1,0:T(4,128)S(1)}, u32[]{:S(2)}) copy-start(f32[4,4,512]{2,1,0:T(4,128)S(1)} %get-tuple-element.16) | copy-start | bytes 98308
Sparse Core Ops, SparseCore 0:
  10.1 33.7 all-gather.1
  441.1 164.8 all-reduce.3
